TPU v7x, 256 devices: a whole 4x4x8 slice. The times are simulated.
256 devices in a mesh: rep: 16 (over x, y), mem: 16 (over z, core).
Axes of the slice: x: 4, y: 4, z: 8, core: 2. Of those that a mesh axis runs over, the one named last changes fastest.
Arguments:
- schur_blocks: bfloat16 [512, 1024, 1024], P(('rep', 'mem')), as said below
- rigid_modes: float32 [512, 6, 1024], P(('rep', 'mem')), may hold values from -0.25 to 0.25
- coarse_inverse: float32 [768, 768], P(None, 'mem'), as said below
- coarse_rhs: float32 [16, 768], P(None, 'mem'), may hold values from -18 to 18
- subdomain_rhs: float32 [16, 512, 1024], P(None, ('rep', 'mem'))
- partner: int32 [512, 8], P(('rep', 'mem')), may hold values from 0 to 4095, as said below
- cluster_of: int32 [512], P(('rep', 'mem')), may hold values from 0 to 127, as said below
Outputs:
- multipliers: float32 [16, 512, 1024], P(None, ('rep', 'mem'))
- projected: float32 [16, 512, 1024], P(None, ('rep', 'mem'))
Inputs may be any that keep to these rules, and one draw needn't show every extreme that they name: partner pairs slots: partner[partner[i]] = i and partner[i] != i over the flattened slots i = 8 * s + j. A slot's partner lies on a device with the same rep index whose mem index equals its own or differs from it in exactly one bit. Two different devices share at most 4 paired slots, and in every rep group some two devices share exactly 4. `cluster_of`: each cluster holds exactly 4 subdomains. `schur_blocks`: each subdomain's block is symmetric. `coarse_inverse`: Symmetric.
All inputs are finite; a program needn't handle non-finite values.
Results may differ from a plain program's by a relative error of at most 0.0003.
Values sent between devices are 32-bit elements; how exact they have to be, the bound alone decides.
A program may use at most 64 MiB of HBM per device.

v0:
```python
import jax
import jax.numpy as jnp
from jax import lax
from jax.sharding import PartitionSpec as P

MODES = 6
ITERS = 2


precise = lax.Precision.HIGHEST


def from_partner(value, axis, bit):
    return lax.ppermute(value, axis, [(i, i ^ 1 << bit) for i in range(lax.axis_size(axis))])


def rank_within(target, ordering):
    same_target = target[:, None] == target[None, :]
    earlier = ordering[None, :] < ordering[:, None]
    return jnp.sum(jnp.logical_and(same_target, earlier).astype(jnp.int32), axis=1)


def inner_sum(first, second):
    return 0.5 * jnp.sum(first * second, axis=(1, 2))


def local(
    schur_blocks, rigid_modes, coarse_inverse, coarse_rhs, subdomain_rhs, partner, cluster_of
):
    sub_count = schur_blocks.shape[0]
    order_lam = schur_blocks.shape[1]
    case_count = subdomain_rhs.shape[0]
    blocks = partner.shape[1]
    block_rows = order_lam // blocks
    slot_count = sub_count * blocks
    capacity = slot_count // 4
    coarse_total = coarse_inverse.shape[0]
    slice_cols = coarse_inverse.shape[1]
    cluster_total = coarse_total // MODES
    slice_clusters = slice_cols // MODES
    mem_size = lax.axis_size("mem")
    mem_index = lax.axis_index("mem")
    device = lax.axis_index("rep") * mem_size + mem_index
    slot_range = jnp.arange(slot_count, dtype=jnp.int32)
    partner_flat = partner.reshape(slot_count)
    slot_ids = device * slot_count + slot_range
    signs = jnp.where(slot_ids < partner_flat, 1.0, -1.0).astype(jnp.float32)
    sign_rows = jnp.broadcast_to(
        signs.reshape(sub_count, blocks, 1), (sub_count, blocks, block_rows)
    ).reshape(sub_count, order_lam)
    target = partner_flat // slot_count % mem_size
    partner_slot = partner_flat % slot_count
    send_rank = rank_within(target, partner_slot)
    recv_rank = rank_within(target, slot_range)
    is_local = target == mem_index
    local_onehot = jnp.logical_and(
        is_local[:, None], partner_slot[:, None] == slot_range[None, :]
    ).astype(jnp.float32)

    def assemble(contributions):
        row_count = contributions.shape[0]
        signed = contributions.reshape(row_count, slot_count, block_rows) * signs[None, :, None]
        received = jnp.einsum("st,ktb->ksb", local_onehot, signed, precision=precise)
        cap_range = jnp.arange(capacity, dtype=jnp.int32)
        for bit_index in range(mem_size.bit_length() - 1):
            peer_index = jnp.bitwise_xor(mem_index, 1 << bit_index)
            to_peer = target == peer_index
            send_onehot = jnp.logical_and(
                to_peer[None, :], send_rank[None, :] == cap_range[:, None]
            ).astype(jnp.float32)
            recv_onehot = jnp.logical_and(
                to_peer[:, None], recv_rank[:, None] == cap_range[None, :]
            ).astype(jnp.float32)
            outgoing = jnp.einsum("ps,ksb->pkb", send_onehot, signed, precision=precise)
            incoming = from_partner(outgoing, "mem", bit_index)
            received = received + jnp.einsum(
                "sp,pkb->ksb", recv_onehot, incoming, precision=precise
            )
        return (signed + received).reshape(row_count, sub_count, order_lam)

    def schur_apply(vector):
        flipped = (vector * sign_rows[None]).astype(jnp.bfloat16)
        local_terms = jnp.einsum(
            "sij,csj->csi", schur_blocks, flipped, preferred_element_type=jnp.float32
        )
        return assemble(local_terms)

    def coarse_slice(vector):
        partials = jnp.einsum(
            "smj,csj->csm", rigid_modes, vector * sign_rows[None], precision=precise
        )
        all_parts, all_ids = (
            lax.all_gather(partials, ("rep", "mem"), axis=1, tiled=True),
            lax.all_gather(cluster_of, ("rep", "mem"), axis=0, tiled=True),
        )
        wanted = mem_index * slice_clusters + jnp.arange(slice_clusters, dtype=jnp.int32)
        selector = (all_ids[None, :] == wanted[:, None]).astype(jnp.float32)
        summed = jnp.einsum("ks,csm->ckm", selector, all_parts, precision=precise)
        return summed.reshape(case_count, slice_cols)

    def coarse_solve(slice_vec):
        partial_sol = jnp.einsum("ab,cb->ca", coarse_inverse, slice_vec, precision=precise)
        return lax.psum(partial_sol, "mem")

    def spread_terms(solution):
        per_cluster = solution.reshape(case_count, cluster_total, MODES)
        picker = (
            cluster_of[:, None] == jnp.arange(cluster_total, dtype=jnp.int32)[None, :]
        ).astype(jnp.float32)
        own_rows = jnp.einsum("sk,ckm->csm", picker, per_cluster, precision=precise)
        return jnp.einsum("smj,csm->csj", rigid_modes, own_rows, precision=precise)

    def project(vector):
        return vector - assemble(spread_terms(coarse_solve(coarse_slice(vector))))

    def norm_total(vector):
        return lax.psum(inner_sum(vector, vector), ("rep", "mem"))

    start_terms = spread_terms(coarse_solve(coarse_rhs))
    both = assemble(jnp.concatenate([subdomain_rhs, start_terms], axis=0))
    dual_rhs = both[:case_count]
    multipliers = both[case_count:]
    residual = dual_rhs - schur_apply(multipliers)
    projected = project(residual)
    norm_now = norm_total(projected)
    direction = projected
    for iteration in range(ITERS):
        curved = schur_apply(direction)
        curvature = lax.psum(inner_sum(direction, curved), ("rep", "mem"))
        step_size = norm_now / curvature
        multipliers = multipliers + step_size[:, None, None] * direction
        residual = residual - step_size[:, None, None] * curved
        projected = project(residual)
        if iteration + 1 < ITERS:
            norm_next = norm_total(projected)
            direction = projected + (norm_next / norm_now)[:, None, None] * direction
            norm_now = norm_next
    return (multipliers, projected)


def solution(mesh):
    placed = (
        P(("rep", "mem"), None, None),
        P(("rep", "mem"), None, None),
        P(None, "mem"),
        P(None, "mem"),
        P(None, ("rep", "mem"), None),
        P(("rep", "mem"), None),
        P(("rep", "mem")),
    )
    return jax.shard_map(
        local,
        mesh=mesh,
        in_specs=placed,
        out_specs=(P(None, ("rep", "mem"), None), P(None, ("rep", "mem"), None)),
        check_vma=False,
    )
```

profile of v0, /device:TPU:1, one launch (start us, length us, event | category | flops | bytes accessed | tf_op | source)
XLA Modules:
  0.0 791.6 jit_solution(12440159952689921085)
XLA Ops:
  4.2 48.9 %psum.56 = f32[16,128,6]{1,0,2:T(8,128)S(1)} all-reduce(f32[16,128,6]{1,0,2:T(8,128)S(1)} %copy.46), channel_id=1, replica_groups=mesh['rep'=16,'mem'=16] {'mem'}, use_global_device_ids=true, to_apply=%region_0.1 | all-reduce | flops 12288 | bytes 98304 | tf_op jit(solution)/shard_map/psum | solution.py:103
  54.8 1.8 collective-permute-start.3
  58.3 3.3 collective-permute-start.1
  62.3 79.4 %all-reduce = s32[512]{0:T(512)S(1)} all-reduce(s32[512]{0:T(512)S(1)} %dynamic-update-slice), channel_id=1, replica_groups=mesh['rep'=16,'mem'=16] {'rep','mem'}, use_global_device_ids=true, to_apply=%add | all-reduce | flops 512 | bytes 4096
  143.6 3.4 convolution_bitcast_fusion.5
  149.5 2.2 collective-permute-start.7
  152.7 4.0 collective-permute-done.6
  158.1 67.3 %all_gather.14 = f32[16,512,6]{0,2,1:T(8,128)S(1)} all-gather(f32[16,2,6]{0,2,1:T(8,128)S(1)} %convolution_bitcast_fusion.9), channel_id=1, replica_groups=mesh['rep'=16,'mem'=16] {'rep','mem'}, dimensions={1}, use_global_device_ids=true | all-gather | bytes 197376 | tf_op jit(solution)/shard_map/all_gather | solution.py:93
  227.2 43.0 %psum.57 = f32[16,128,6]{1,0,2:T(8,128)S(1)} all-reduce(f32[16,128,6]{1,0,2:T(8,128)S(1)} %copy.58), channel_id=1, replica_groups=mesh['rep'=16,'mem'=16] {'mem'}, use_global_device_ids=true, to_apply=%region_3.4 | all-reduce | flops 12288 | bytes 98304 | tf_op jit(solution)/shard_map/psum | solution.py:103
  272.0 3.6 collective-permute-start.8
  275.9 3.5 collective-permute-start.11
  279.7 3.7 collective-permute-done.10
  284.4 3.4 convolution_bitcast_fusion.3
  290.5 2.8 collective-permute-start.15
  294.7 3.2 collective-permute-done.14
  299.0 74.5 %all-reduce.1 = (f32[16]{0:T(128)S(1)}, f32[16]{0:T(128)S(1)}) all-reduce(f32[16]{0:T(128)S(1)} %get-tuple-element.36, f32[16]{0:T(128)S(1)} %get-tuple-element.35), channel_id=1, replica_groups=mesh['rep'=16,'mem'=16] {'rep','mem'}, use_global_device_ids=true, to_apply=%region_5.6 | all-reduce | flops 32 | bytes 256 | tf_op jit(solution)/shard_map/psum | solution.py:117
  373.9 67.1 %all_gather.16 = f32[16,512,6]{0,2,1:T(8,128)S(1)} all-gather(f32[16,2,6]{0,2,1:T(8,128)S(1)} %convolution_bitcast_fusion.8), channel_id=1, replica_groups=mesh['rep'=16,'mem'=16] {'rep','mem'}, dimensions={1}, use_global_device_ids=true | all-gather | bytes 197376 | tf_op jit(solution)/shard_map/all_gather | solution.py:93
  442.8 43.1 %psum.60 = f32[16,128,6]{1,0,2:T(8,128)S(1)} all-reduce(f32[16,128,6]{1,0,2:T(8,128)S(1)} %copy.69), channel_id=1, replica_groups=mesh['rep'=16,'mem'=16] {'mem'}, use_global_device_ids=true, to_apply=%region_8.9 | all-reduce | flops 12288 | bytes 98304 | tf_op jit(solution)/shard_map/psum | solution.py:103
  487.9 3.6 collective-permute-start.16
  491.8 2.9 collective-permute-start.19
  494.9 3.7 collective-permute-done.18
  499.6 74.1 %psum.61 = f32[16]{0:T(128)S(1)} all-reduce(f32[16]{0:T(128)S(1)} %broadcast_multiply_fusion.4), channel_id=1, replica_groups=mesh['rep'=16,'mem'=16] {'rep','mem'}, use_global_device_ids=true, to_apply=%region_10.11 | all-reduce | flops 16 | bytes 128 | tf_op jit(solution)/shard_map/psum | solution.py:117
  574.0 3.4 convolution_bitcast_fusion.1
  579.6 2.9 collective-permute-start.23
  582.7 2.0 collective-permute-start.21
  585.0 1.8 collective-permute-done.22
  588.6 74.4 %psum.62 = f32[16]{0:T(128)S(1)} all-reduce(f32[16]{0:T(128)S(1)} %broadcast_multiply_fusion.3), channel_id=1, replica_groups=mesh['rep'=16,'mem'=16] {'rep','mem'}, use_global_device_ids=true, to_apply=%region_12.13 | all-reduce | flops 16 | bytes 128 | tf_op jit(solution)/shard_map/psum | solution.py:129
  663.5 66.9 %all_gather.17 = f32[16,512,6]{0,2,1:T(8,128)S(1)} all-gather(f32[16,2,6]{0,2,1:T(8,128)S(1)} %convolution_bitcast_fusion.7), channel_id=1, replica_groups=mesh['rep'=16,'mem'=16] {'rep','mem'}, dimensions={1}, use_global_device_ids=true | all-gather | bytes 197376 | tf_op jit(solution)/shard_map/all_gather | solution.py:93
  732.1 45.0 %psum.63 = f32[16,128,6]{1,0,2:T(8,128)S(1)} all-reduce(f32[16,128,6]{1,0,2:T(8,128)S(1)} %copy.80), channel_id=1, replica_groups=mesh['rep'=16,'mem'=16] {'mem'}, use_global_device_ids=true, to_apply=%region_13.14 | all-reduce | flops 12288 | bytes 98304 | tf_op jit(solution)/shard_map/psum | solution.py:103
  779.0 3.6 collective-permute-start.24
  782.8 2.3 collective-permute-start.27
  785.5 3.4 collective-permute-done.26
  (194 shorter events, 41.5 us)
Async XLA Ops:
  0.6 1.9 copy-start
  0.6 52.5 %copy-start.3 = (s32[2]{0:T(128)S(1)}, s32[2]{0:T(128)}, u32[]{:S(2)}) copy-start(s32[2]{0:T(128)} %param.13) | copy-start | bytes 28
  0.7 52.8 %copy-start.1 = (f32[2,6,1024]{2,0,1:T(2,128)S(1)}, f32[2,6,1024]{2,0,1:T(2,128)}, u32[]{:S(2)}) copy-start(f32[2,6,1024]{2,0,1:T(2,128)} %param.8) | copy-start | bytes 147460
  4.1 57.9 %copy-start.2 = (s32[2,8]{1,0:T(2,128)S(1)}, s32[2,8]{1,0:T(2,128)}, u32[]{:S(2)}) copy-start(s32[2,8]{1,0:T(2,128)} %param.12) | copy-start | bytes 196
  54.8 87.9 %collective-permute-start.3 = (f32[4,32,128]{2,0,1:T(4,128)S(1)}, f32[4,32,128]{2,0,1:T(4,128)S(1)}, u32[]{:S(2)}, u32[]{:S(2)}) collective-permute-start(f32[4,32,128]{2,0,1:T(4,128)S(1)} %fusion.43), channel_id=1, source_target_pairs={{0,8},{1,9},{2,10},{3,11},{4,12},{5,13},{6,14},{7,15},{8,0},{9,1},... | collective-permute-start | bytes 196616 | tf_op jit(solution)/shard_map/ppermute | solution.py:14
  56.9 85.5 %collective-permute-start.2 = (f32[4,32,128]{2,0,1:T(4,128)S(1)}, f32[4,32,128]{2,0,1:T(4,128)S(1)}, u32[]{:S(2)}, u32[]{:S(2)}) collective-permute-start(f32[4,32,128]{2,0,1:T(4,128)S(1)} %fusion.45), channel_id=1, source_target_pairs={{0,4},{1,5},{2,6},{3,7},{4,0},{5,1},{6,2},{7,3},{8,12},{9,13},{10,... | collective-permute-start | bytes 196616 | tf_op jit(solution)/shard_map/ppermute | solution.py:14
  58.3 84.8 %collective-permute-start.1 = (f32[4,32,128]{2,0,1:T(4,128)S(1)}, f32[4,32,128]{2,0,1:T(4,128)S(1)}, u32[]{:S(2)}, u32[]{:S(2)}) collective-permute-start(f32[4,32,128]{2,0,1:T(4,128)S(1)} %fusion.47), channel_id=1, source_target_pairs={{0,2},{1,3},{2,0},{3,1},{4,6},{5,7},{6,4},{7,5},{8,10},{9,11},{10,... | collective-permute-start | bytes 196616 | tf_op jit(solution)/shard_map/ppermute | solution.py:14
  61.9 80.2 %collective-permute-start = (f32[4,32,128]{2,0,1:T(4,128)S(1)}, f32[4,32,128]{2,0,1:T(4,128)S(1)}, u32[]{:S(2)}, u32[]{:S(2)}) collective-permute-start(f32[4,32,128]{2,0,1:T(4,128)S(1)} %fusion.49), channel_id=1, source_target_pairs={{0,1},{1,0},{2,3},{3,2},{4,5},{5,4},{6,7},{7,6},{8,9},{9,8},{10,11... | collective-permute-start | bytes 196616 | tf_op jit(solution)/shard_map/ppermute | solution.py:14
  148.2 4.3 collective-permute-start.4
  149.5 7.7 collective-permute-start.7
  151.7 5.1 collective-permute-start.6
  151.7 5.8 collective-permute-start.5
  272.0 7.4 collective-permute-start.8
  275.9 7.7 collective-permute-start.11
  279.4 4.0 collective-permute-start.10
  279.4 4.5 collective-permute-start.9
  289.0 5.4 collective-permute-start.12
  290.5 7.7 collective-permute-start.15
  293.3 4.6 collective-permute-start.14
  293.8 4.6 collective-permute-start.13
  487.9 6.7 collective-permute-start.16
  491.8 7.1 collective-permute-start.19
  494.6 4.0 collective-permute-start.18
  494.6 4.5 collective-permute-start.17
  578.6 6.1 collective-permute-start.20
  579.6 7.4 collective-permute-start.23
  582.4 4.3 collective-permute-start.22
  582.7 5.3 collective-permute-start.21
  779.0 6.3 collective-permute-start.24
  782.8 6.8 collective-permute-start.27
  785.2 3.8 collective-permute-start.26
  785.2 4.7 collective-permute-start.25
where the time goes:
time: 801 us; the launch traced here: 792 us
  blocking collectives  684 us (85%)
  starting transfers between devices  41.1 us (5%)
  matrix products  36.3 us (5%)
  waiting for transfers between devices  21.1 us (3%)
    all_gather x3, blocking collectives, coarse_slice(): lax.all_gather(partials, ('rep', 'mem'), axis=1, tiled=True)  201 us
    psum x4, blocking collectives, coarse_solve(): return lax.psum(partial_sol, 'mem')  180 us
    psum x2, blocking collectives, norm_total(): return lax.psum(inner_sum(vector, vector), ('rep', 'mem'))  149 us
    unnamed x1, blocking collectives  79.4 us
    psum x1, blocking collectives, local(): curvature = lax.psum(inner_sum(direction, curved), ('rep', 'mem'))  74.4 us
    ppermute x28, starting transfers between devices, from_partner(): lax.ppermute(value, axis, [(i, i ^ 1 << bit) for i in range(lax.axis_size...  41.1 us
    ppermute x28, waiting for transfers between devices, from_partner(): lax.ppermute(value, axis, [(i, i ^ 1 << bit) for i in range(lax.axis_size...  21.1 us
  transfers between devices with their start and end apart: 28, of which 9 were waited for; matrix products, arithmetic and copies ran while one was open for 1% of the time, Pallas kernels for 0%

commit v1 on v0

v1 whole, which is shorter than its diff:
```python
import functools

import jax
import jax.numpy as jnp
from jax import lax
from jax.experimental import pallas as pl
from jax.experimental.pallas import tpu as pltpu
from jax.sharding import PartitionSpec as P

MESH = pl.DeviceIdType.MESH
F32 = jnp.float32
BF = jnp.bfloat16
CASES = 16
MODES = 6
SLOTS = 16
LANES = 128
ENT = 144
STEPS = 3


def split3(x):
    hi = x.astype(BF)
    rest = x - hi.astype(F32)
    mid = rest.astype(BF)
    low = (rest - mid.astype(F32)).astype(BF)
    return hi, mid, low


def mm(a, b, nt=False):
    return lax.dot_general(
        a, b, (((1,), (1 if nt else 0,)), ((), ())), preferred_element_type=F32
    )


def dot3(x, w, nt=False):
    n = x.shape[0]
    a = jnp.concatenate(split3(x), axis=0)
    r1 = mm(a, w[0], nt)
    r2 = mm(a[: 2 * n], w[1], nt)
    r3 = mm(a[:n], w[2], nt)
    return r1[:n] + ((r1[n : 2 * n] + r2[:n]) + (r1[2 * n :] + r2[n:] + r3))


def dot_exact(x, onehot, nt=False):
    n = x.shape[0]
    r = mm(jnp.concatenate(split3(x), axis=0), onehot, nt)
    return r[:n] + (r[n : 2 * n] + r[2 * n :])


def total16(ref, *lead):
    parts = [ref[(*lead, i)] for i in range(16)]
    while len(parts) > 1:
        parts = [a + b for a, b in zip(parts[::2], parts[1::2])]
    return parts[0]


def kernel(
    n_rep, n_mem,
    partner_ref, cluster_ref, modes_ref, qinv_ref, crhs_ref, rhs_ref, schur_hbm,
    out_l, out_p,
    kbuf, wt, qpad, qp, qn, sc, scy,
    gall, gown, gsend, tall0, tall1, tall2, town, tsend,
    crpad, crall, yall, eb, rs, ra, gb,
    tm, tr,
    lam, p0, p1, d1,
    key, code, pos, sslot, sgn,
    ksem, send, recv,
):
    rep = lax.axis_index("rep")
    mem = lax.axis_index("mem")
    kcopy = pltpu.make_async_copy(schur_hbm, kbuf, ksem)
    kcopy.start()
    bar = pltpu.get_barrier_semaphore()

    def greet(axis, me, n):
        def body(off, _):
            pl.semaphore_signal(
                bar, inc=1, device_id={axis: me ^ off}, device_id_type=MESH
            )
            return 0
        lax.fori_loop(1, n, body, 0)

    greet("mem", mem, n_mem)
    greet("rep", rep, n_rep)

    def remote(src, dst, r, axis, peer):
        return pltpu.make_async_remote_copy(
            src_ref=src, dst_ref=dst, send_sem=send.at[r], recv_sem=recv.at[r],
            device_id={axis: peer}, device_id_type=MESH,
        )

    def scatter(src_of, dst, r, axis, me, n):
        def body(off, _):
            peer = me ^ off
            remote(src_of(peer), dst.at[me], r, axis, peer).start()
            return 0
        lax.fori_loop(1, n, body, 0)

    def finish(dst, r, axis, me, n):
        most = dst.at[pl.ds(0, n - 1)]
        copy = remote(most, most, r, axis, me ^ 1)
        copy.wait_recv()
        return copy

    def exchange_start(src, dst, r):
        for bit in range(4):
            remote(
                src.at[pl.ds(4 * bit, 4)], dst.at[pl.ds(SLOTS + 4 * bit, 4)],
                r, "mem", mem ^ (1 << bit),
            ).start()

    def exchange_wait(src, dst, r):
        copy = remote(src, dst.at[pl.ds(SLOTS, SLOTS)], r, "mem", mem ^ 1)
        copy.wait_recv()
        return copy

    for i in range(SLOTS):
        value = partner_ref[i // 8, i % 8]
        key[i] = value & (16 * n_mem - 1)
        first = (rep * n_mem + mem) * SLOTS + i < value
        sgn[i] = jnp.where(first, 1.0, -1.0).astype(F32)

    def table(i, _):
        mine = key[i]
        base = mine & ~15
        sent = jnp.int32(0)
        got = jnp.int32(0)
        for k in range(SLOTS):
            other = key[k]
            same = (other & ~15) == base
            sent += jnp.where(jnp.logical_and(same, other < mine), 1, 0)
            got += jnp.where(jnp.logical_and(same, i > k), 1, 0)
        diff = (mine >> 4) ^ mem
        bit = (
            jnp.where(diff >= 2, 4, 0) + jnp.where(diff >= 4, 4, 0)
            + jnp.where(diff >= 8, 4, 0)
        )
        here = diff == 0
        code[i] = jnp.where(here, -1, bit + sent)
        pos[i] = jnp.where(here, mine & 15, SLOTS + bit + (got & 3))
        return 0
    lax.fori_loop(0, SLOTS, table, 0)

    def places(p, _):
        found = jnp.int32(0)
        for k in range(SLOTS):
            found += jnp.where(code[k] == p, k, 0)
        sslot[p] = found & 15
        return 0
    lax.fori_loop(0, SLOTS, places, 0)

    for i in range(SLOTS):
        s, j = divmod(i, 8)
        for own in (gown, gall):
            own[i, 0:MODES, :] = modes_ref[s, :, LANES * j : LANES * (j + 1)]
            own[i, MODES:8, :] = jnp.full((2, LANES), cluster_ref[s].astype(F32), F32)
    for p in range(SLOTS):
        gsend[p] = gown[sslot[p]]

    odd = (mem & 1) == 1
    crpad[...] = jnp.zeros_like(crpad)
    crpad[:, 0:48] = crhs_ref[...]
    place = crpad[...]
    crall[mem] = jnp.where(odd, pltpu.roll(place, 64, 1), place)

    pl.semaphore_wait(bar, n_mem + n_rep - 2)

    pending = []
    scatter(lambda peer: crall.at[mem], crall, 0, "mem", mem, n_mem)
    exchange_start(gsend, gall, 1)

    qpad[...] = jnp.zeros_like(qpad)
    qpad[:, 0:48] = qinv_ref[...]
    place = qpad[...]
    qpad[...] = jnp.where(odd, pltpu.roll(place, 64, 1), place)
    qn[...] = jnp.zeros_like(qn)
    for m in range(16):
        parts = split3(qpad[48 * m : 48 * (m + 1), :])
        for t in range(3):
            qn[t, 64 * m : 64 * m + 48, :] = parts[t]
    for m in range(MODES):
        parts = split3(qpad[pl.ds(m, LANES, stride=MODES), :])
        for t in range(3):
            qp[t, LANES * m : LANES * (m + 1), :] = parts[t]
    wt[...] = jnp.zeros_like(wt)

    row = lax.broadcasted_iota(jnp.int32, (8, LANES), 0)
    blank = jnp.zeros((8, LANES), F32)

    def store_modes(i, half, first_row, tile):
        tile = jnp.where(row < MODES, tile, 0.0)
        both = [blank, tile] if half else [tile, blank]
        parts = split3(jnp.concatenate(both, axis=0))
        for t in range(3):
            wt[t, first_row : first_row + 16, LANES * i : LANES * (i + 1)] = parts[t]

    for i in range(SLOTS):
        store_modes(i, i // 8, 128, gown[i])

    pending.append(exchange_wait(gsend, gall, 1))
    ids = []
    for i in range(SLOTS):
        got = gall[pos[i]]
        store_modes(i, i % 2, 16 * (i // 2), -got)
        ids.append(jnp.broadcast_to(got[MODES : MODES + 1, :], (8, LANES)))
    for s in range(2):
        ids.append(jnp.full((8, LANES), cluster_ref[s].astype(F32), F32))

    lane = lax.broadcasted_iota(jnp.int32, (16, LANES), 1)
    mode = lax.broadcasted_iota(jnp.int32, (16, LANES), 0) & 7
    lane_f = lane.astype(F32)
    in_half = lane & 63
    sub = (in_half * 43) >> 8
    sub_mode = in_half - MODES * sub
    fits = jnp.logical_and(in_half < 48, sub_mode == mode)
    first_cluster = (sub + 8 * (lane >> 6)).astype(F32)
    for a in range(9):
        pair = jnp.concatenate([ids[2 * a], ids[2 * a + 1]], axis=0)
        rows = slice(16 * a, 16 * (a + 1))
        for m in range(MODES):
            hit = jnp.logical_and(mode == m, lane_f == pair)
            sc[rows, LANES * m : LANES * (m + 1)] = jnp.where(hit, 1.0, 0.0).astype(BF)
        for j in range(8):
            hit = jnp.logical_and(fits, first_cluster + 16.0 * j == pair)
            scy[rows, LANES * j : LANES * (j + 1)] = jnp.where(hit, 1.0, 0.0).astype(BF)

    def pairs(ref):
        return jnp.concatenate(
            [ref[2 * j] + ref[2 * j + 1] for j in range(8)], axis=1
        )

    def spread(y_slice, step):
        y = yall.at[step]
        r = 2 + step
        y[mem] = y_slice
        scatter(lambda peer: y.at[mem], y, r, "mem", mem, n_mem)
        pending.append(finish(y, r, "mem", mem, n_mem))
        picked = dot_exact(pairs(y), scy[...], nt=True)
        return dot3(picked, (wt[0], wt[1], wt[2]))

    def schur(src):
        out = []
        for s in range(2):
            flat = jnp.concatenate(
                [src[8 * s + j].astype(BF) for j in range(8)], axis=1
            )
            out.append(mm(flat, kbuf[s]))
        return out

    def lanes_of(values, i):
        return values[:, LANES * i : LANES * (i + 1)]

    def reduce_start(step, scalars):
        t = (tall0, tall1, tall2)[step]
        e = eb.at[step]
        base = 6 + 4 * step
        for i in range(SLOTS):
            t[i] = town[step, i]
        flat = jnp.concatenate([town[step, i] for i in range(SLOTS)], axis=1)
        own = dot3(flat, (wt[0], wt[1], wt[2]), nt=True)
        dense = dot_exact(own, sc[...])
        for m in range(MODES):
            e[:, m, :] = lanes_of(dense, m)
        for k, value in enumerate(scalars):
            e[:, MODES + k, :] = value
        rs[step, mem] = e[mem]
        scatter(lambda peer: e.at[peer], rs.at[step], base, "mem", mem, n_mem)
        for p in range(SLOTS):
            tsend[step, p] = town[step, sslot[p]]
        exchange_start(tsend.at[step], t, base + 1)
        pending.append(finish(rs.at[step], base, "mem", mem, n_mem))
        ra[step, rep] = total16(rs, step)
        scatter(lambda peer: ra.at[step, rep], ra.at[step], base + 2, "rep", rep, n_rep)
        pending.append(finish(ra.at[step], base + 2, "rep", rep, n_rep))
        g = gb.at[step]
        g[mem] = total16(ra, step)
        scatter(lambda peer: g.at[mem], g, base + 3, "mem", mem, n_mem)
        pending.append(finish(g, base + 3, "mem", mem, n_mem))
        e_full = jnp.concatenate([g[:, m, :] for m in range(MODES)], axis=1)
        z = spread(dot3(e_full, (qp[0], qp[1], qp[2])), 1 + step)
        pending.append(exchange_wait(tsend.at[step], t, base + 1))
        return [
            (t[i] - t[pos[i]]) - lanes_of(z, i) for i in range(SLOTS)
        ]

    def lane_sum(x):
        return jnp.sum(x, axis=1, keepdims=True)

    pending.append(finish(crall, 0, "mem", mem, n_mem))
    z = spread(dot3(pairs(crall), (qn[0], qn[1], qn[2])), 0)
    for i in range(SLOTS):
        lam[i] = lanes_of(z, i)
    kcopy.wait()
    zero = jnp.zeros((CASES, LANES), F32)
    terms = schur(lam)
    for i in range(SLOTS):
        s, j = divmod(i, 8)
        cut = slice(LANES * j, LANES * (j + 1))
        town[0, i] = rhs_ref[:, s, cut] - terms[s][:, cut]
    projected = reduce_start(0, (zero, zero))
    square = zero
    for i in range(SLOTS):
        p0[i] = projected[i]
        square = square + projected[i] * projected[i]

    terms = schur(p0)
    curve = zero
    for i in range(SLOTS):
        s, j = divmod(i, 8)
        value = terms[s][:, LANES * j : LANES * (j + 1)]
        town[1, i] = value
        curve = curve + value * p0[i]
    image = reduce_start(1, (curve, square))
    curvature = lane_sum(gb[1, :, MODES, :])
    norm = 0.5 * lane_sum(gb[1, :, MODES + 1, :])
    alpha = norm / curvature
    square = zero
    for i in range(SLOTS):
        value = p0[i] - alpha * image[i]
        p1[i] = value
        lam[i] = lam[i] + alpha * p0[i]
        square = square + value * value
    diagonal = lax.broadcasted_iota(jnp.int32, (CASES, LANES), 0) == lane
    as_row = jnp.sum(
        jnp.where(diagonal, lane_sum(square), 0.0), axis=0, keepdims=True
    )
    tm[mem] = as_row
    scatter(lambda peer: tm.at[mem], tm, 18, "mem", mem, n_mem)
    pending.append(finish(tm, 18, "mem", mem, n_mem))
    tr[rep] = total16(tm)
    scatter(lambda peer: tr.at[rep], tr, 19, "rep", rep, n_rep)
    pending.append(finish(tr, 19, "rep", rep, n_rep))
    fresh = 0.5 * lane_sum(
        jnp.where(diagonal, jnp.broadcast_to(total16(tr), (CASES, LANES)), 0.0)
    )
    beta = fresh / norm
    for i in range(SLOTS):
        d1[i] = p1[i] + beta * p0[i]

    terms = schur(d1)
    curve = zero
    for i in range(SLOTS):
        s, j = divmod(i, 8)
        value = terms[s][:, LANES * j : LANES * (j + 1)]
        town[2, i] = value
        curve = curve + value * d1[i]
    image = reduce_start(2, (curve, zero))
    alpha = fresh / lane_sum(gb[2, :, MODES, :])
    for i in range(SLOTS):
        s, j = divmod(i, 8)
        cut = slice(LANES * j, LANES * (j + 1))
        out_l[:, s, cut] = sgn[i] * (lam[i] + alpha * d1[i])
        out_p[:, s, cut] = sgn[i] * (p1[i] - alpha * image[i])

    for copy in pending:
        copy.wait_send()


def local(
    n_rep, n_mem,
    schur_blocks, rigid_modes, coarse_inverse, coarse_rhs, subdomain_rhs, partner, cluster_of,
):
    vmem = pl.BlockSpec(memory_space=pltpu.VMEM)
    smem = pl.BlockSpec(memory_space=pltpu.SMEM)
    out = jax.ShapeDtypeStruct((CASES, 2, 1024), F32)
    tile = (CASES, LANES)
    return pl.pallas_call(
        functools.partial(kernel, n_rep, n_mem),
        out_shape=(out, out),
        in_specs=[smem, smem, vmem, vmem, vmem, vmem, pl.BlockSpec(memory_space=pl.ANY)],
        out_specs=(vmem, vmem),
        scratch_shapes=[
            pltpu.VMEM((2, 1024, 1024), BF),
            pltpu.VMEM((3, ENT, 2048), BF),
            pltpu.VMEM((768, LANES), F32),
            pltpu.VMEM((3, 768, LANES), BF),
            pltpu.VMEM((3, 1024, LANES), BF),
            pltpu.VMEM((ENT, 768), BF),
            pltpu.VMEM((ENT, 1024), BF),
            pltpu.VMEM((2 * SLOTS, 8, LANES), F32),
            pltpu.VMEM((SLOTS, 8, LANES), F32),
            pltpu.VMEM((SLOTS, 8, LANES), F32),
            pltpu.VMEM((2 * SLOTS, *tile), F32),
            pltpu.VMEM((2 * SLOTS, *tile), F32),
            pltpu.VMEM((2 * SLOTS, *tile), F32),
            pltpu.VMEM((STEPS, SLOTS, *tile), F32),
            pltpu.VMEM((STEPS, SLOTS, *tile), F32),
            pltpu.VMEM(tile, F32),
            pltpu.VMEM((16, *tile), F32),
            pltpu.VMEM((1 + STEPS, 16, *tile), F32),
            pltpu.VMEM((STEPS, CASES, 8, LANES), F32),
            pltpu.VMEM((STEPS, 16, 8, LANES), F32),
            pltpu.VMEM((STEPS, 16, 8, LANES), F32),
            pltpu.VMEM((STEPS, 16, 8, LANES), F32),
            pltpu.VMEM((16, 1, LANES), F32),
            pltpu.VMEM((16, 1, LANES), F32),
            pltpu.VMEM((SLOTS, *tile), F32),
            pltpu.VMEM((SLOTS, *tile), F32),
            pltpu.VMEM((SLOTS, *tile), F32),
            pltpu.VMEM((SLOTS, *tile), F32),
            pltpu.SMEM((SLOTS,), jnp.int32),
            pltpu.SMEM((SLOTS,), jnp.int32),
            pltpu.SMEM((SLOTS,), jnp.int32),
            pltpu.SMEM((SLOTS,), jnp.int32),
            pltpu.SMEM((SLOTS,), F32),
            pltpu.SemaphoreType.DMA,
            pltpu.SemaphoreType.DMA((20,)),
            pltpu.SemaphoreType.DMA((20,)),
        ],
        compiler_params=pltpu.CompilerParams(
            collective_id=0, has_side_effects=True, vmem_limit_bytes=60 * 1024 * 1024
        ),
    )(
        partner, cluster_of, rigid_modes, coarse_inverse, coarse_rhs, subdomain_rhs,
        schur_blocks,
    )


def solution(mesh):
    placed = (
        P(("rep", "mem"), None, None),
        P(("rep", "mem"), None, None),
        P(None, "mem"),
        P(None, "mem"),
        P(None, ("rep", "mem"), None),
        P(("rep", "mem"), None),
        P(("rep", "mem")),
    )
    return jax.shard_map(
        functools.partial(local, mesh.shape["rep"], mesh.shape["mem"]),
        mesh=mesh,
        in_specs=placed,
        out_specs=(P(None, ("rep", "mem"), None), P(None, ("rep", "mem"), None)),
        check_vma=False,
    )
```

time: 801 us -> 116 us (0.14); the launches traced: 792 us -> 116 us
  blocking collectives: 684 us -> 0 us
  Pallas kernels: 0 us -> 109 us
  starting transfers between devices: 41.1 us -> 0 us
  matrix products: 36.3 us -> 0 us
  waiting for transfers between devices: 21.1 us -> 0 us
    psum x7 -> x0, blocking collectives: 403 us -> none  [the longest x4 180 us: coarse_solve(): return lax.psum(partial_sol, 'mem')]
    all_gather x3 -> x0, blocking collectives: 201 us -> none  [coarse_slice(): lax.all_gather(partials, ('rep', 'mem'), axis=1, tiled=True)]
    pallas_call x0 -> x1, Pallas kernels: none -> 109 us  [local(): pl.pallas_call(functools.partial(kernel, n_rep, n_mem), out_shape=(out, o...]
    unnamed x1 -> x0, blocking collectives: 79.4 us -> none
    ppermute x28 -> x0, starting transfers between devices: 41.1 us -> none  [from_partner(): lax.ppermute(value, axis, [(i, i ^ 1 << bit) for i in range(lax.axis_size...]
    dot_general x84 -> x0, matrix products: 36.3 us -> none  [the longest x3 10.1 us: schur_apply(): jnp.einsum('sij,csj->csi', schur_blocks, flipped, preferred_element_type=...]
    ppermute x28 -> x0, waiting for transfers between devices: 21.1 us -> none  [from_partner(): lax.ppermute(value, axis, [(i, i ^ 1 << bit) for i in range(lax.axis_size...]
  transfers between devices with their start and end apart: 28 -> 0, of which waited for: 9 -> 0; matrix products, arithmetic and copies ran while one was open for 1% -> 0% of each run, Pallas kernels for 0% -> 0%
where the time goes in v1:
time: 116 us
  Pallas kernels  109 us (94%)
  local copies, waits for them, and re-layouts  6.39 us (6%)
    pallas_call x1, Pallas kernels, local(): pl.pallas_call(functools.partial(kernel, n_rep, n_mem), out_shape=(out, o...  109 us
    unnamed x4, local copies, waits for them, and re-layouts  6.39 us

profile of v1, /device:TPU:1, one launch (start us, length us, event | category | flops | bytes accessed | tf_op | source)
XLA Modules:
  0.0 116.0 jit_solution(12318846756764483136)
XLA Ops:
  0.6 1.4 %copy.9.modes_ref = f32[2,6,1024]{2,1,0:T(8,128)} copy(f32[2,6,1024]{2,0,1:T(2,128)} %param.8) | data formatting | bytes 98304 | tf_op args[1]
  2.1 1.8 %copy.10.qinv_ref = f32[768,48]{1,0:T(8,128)} copy(f32[768,48]{0,1:T(8,128)} %param.9) | data formatting | bytes 294912 | tf_op args[2]
  3.9 108.9 %shard_map.86 = (f32[16,2,1024]{2,1,0:T(2,128)}, f32[16,2,1024]{2,1,0:T(2,128)}) custom-call(s32[2,8]{1,0:T(2,128)} %partner_ref.1, s32[2]{0:T(128)} %cluster_ref.1, f32[2,6,1024]{2,1,0:T(8,128)} %copy.9.modes_ref, f32[768,48]{1,0:T(8,128)} %copy.10.qinv_ref, f32[16,48]{1,0:T(8,128)} %crhs_ref.1, f32[16,2,1024]{2,1,0:T(2,128)} %rhs_ref.1, ...), custom_call_target="tpu_custom_call" | custom-call | tf_op jit(solution)/shard_map/pallas_call | solution.py:367
  112.8 1.6 %copy.13 = f32[16,2,1024]{2,1,0:T(2,128)} copy(f32[16,2,1024]{2,1,0:T(2,128)} %get-tuple-element.4) | data formatting | bytes 262144
  114.4 1.6 %copy.14 = f32[16,2,1024]{2,1,0:T(2,128)} copy(f32[16,2,1024]{2,1,0:T(2,128)} %get-tuple-element.5) | data formatting | bytes 262144

commit v2 on v1

--- a/solution.py
+++ b/solution.py
@@ -14,7 +14,6 @@
 MODES = 6
 SLOTS = 16
 LANES = 128
-ENT = 144
 STEPS = 3
 
 
@@ -58,12 +57,12 @@
     n_rep, n_mem,
     partner_ref, cluster_ref, modes_ref, qinv_ref, crhs_ref, rhs_ref, schur_hbm,
     out_l, out_p,
-    kbuf, wt, qpad, qp, qn, sc, scy,
+    kbuf, wtf, wt, qf, qp, qs, ball, sc,
     gall, gown, gsend, tall0, tall1, tall2, town, tsend,
-    crpad, crall, yall, eb, rs, ra, gb,
+    crpad, crall, rowall, index_ref, yall, ysend, eb, rs, ra,
     tm, tr,
     lam, p0, p1, d1,
-    key, code, pos, sslot, sgn,
+    key, code, pos, sslot, psub, sgn,
     ksem, send, recv,
 ):
     rep = lax.axis_index("rep")
@@ -90,8 +89,8 @@
         )
 
     def scatter(src_of, dst, r, axis, me, n):
-        def body(off, _):
-            peer = me ^ off
+        def body(k, _):
+            peer = me ^ (n - k)
             remote(src_of(peer), dst.at[me], r, axis, peer).start()
             return 0
         lax.fori_loop(1, n, body, 0)
@@ -103,7 +102,7 @@
         return copy
 
     def exchange_start(src, dst, r):
-        for bit in range(4):
+        for bit in (3, 2, 1, 0):
             remote(
                 src.at[pl.ds(4 * bit, 4)], dst.at[pl.ds(SLOTS + 4 * bit, 4)],
                 r, "mem", mem ^ (1 << bit),
@@ -117,6 +116,7 @@
     for i in range(SLOTS):
         value = partner_ref[i // 8, i % 8]
         key[i] = value & (16 * n_mem - 1)
+        psub[i] = ((value >> 3) & (2 * n_mem - 1)).astype(F32)
         first = (rep * n_mem + mem) * SLOTS + i < value
         sgn[i] = jnp.where(first, 1.0, -1.0).astype(F32)
 
@@ -151,11 +151,21 @@
 
     for i in range(SLOTS):
         s, j = divmod(i, 8)
-        for own in (gown, gall):
-            own[i, 0:MODES, :] = modes_ref[s, :, LANES * j : LANES * (j + 1)]
-            own[i, MODES:8, :] = jnp.full((2, LANES), cluster_ref[s].astype(F32), F32)
+        value = modes_ref[:, s, LANES * j : LANES * (j + 1)]
+        gown[i, 0:MODES, :] = value
+        gall[i, 0:MODES, :] = value
     for p in range(SLOTS):
         gsend[p] = gown[sslot[p]]
+
+    lane1 = lax.broadcasted_iota(jnp.int32, (1, LANES), 1)
+    entry = (lane1 * 43) >> 8
+    row = jnp.full((1, LANES), -1.0, F32)
+    for i in range(SLOTS):
+        row = jnp.where(entry == i, psub[i], row)
+    for s in range(2):
+        row = jnp.where(entry == SLOTS + s, (2 * mem + s).astype(F32), row)
+        row = jnp.where(lane1 == 6 * 18 + s, cluster_ref[s].astype(F32), row)
+    rowall[mem] = row
 
     odd = (mem & 1) == 1
     crpad[...] = jnp.zeros_like(crpad)
@@ -163,80 +173,38 @@
     place = crpad[...]
     crall[mem] = jnp.where(odd, pltpu.roll(place, 64, 1), place)
 
+    parts = split3(qinv_ref[...])
+    for t in range(3):
+        qs[48 * t : 48 * (t + 1), :] = parts[t]
+    qf[...] = jnp.zeros_like(qf)
+    half = pl.ds(pl.multiple_of(64 * (mem & 1), 64), 48)
+    for m in range(16):
+        qf[half, 64 * m : 64 * m + 48] = qinv_ref[:, 48 * m : 48 * (m + 1)]
+    for j in range(8):
+        cut = slice(LANES * j, LANES * (j + 1))
+        parts = split3(qf[:, cut])
+        for t in range(3):
+            qp[t, :, cut] = parts[t]
+    wtf[...] = jnp.zeros_like(wtf)
+    ball[...] = jnp.zeros_like(ball)
+    for i in range(SLOTS):
+        s = i // 8
+        wtf[96 + 6 * s : 102 + 6 * s, LANES * i : LANES * (i + 1)] = gown[i, 0:MODES, :]
+
     pl.semaphore_wait(bar, n_mem + n_rep - 2)
 
     pending = []
     scatter(lambda peer: crall.at[mem], crall, 0, "mem", mem, n_mem)
+    scatter(lambda peer: rowall.at[mem], rowall, 20, "mem", mem, n_mem)
     exchange_start(gsend, gall, 1)
-
-    qpad[...] = jnp.zeros_like(qpad)
-    qpad[:, 0:48] = qinv_ref[...]
-    place = qpad[...]
-    qpad[...] = jnp.where(odd, pltpu.roll(place, 64, 1), place)
-    qn[...] = jnp.zeros_like(qn)
-    for m in range(16):
-        parts = split3(qpad[48 * m : 48 * (m + 1), :])
-        for t in range(3):
-            qn[t, 64 * m : 64 * m + 48, :] = parts[t]
-    for m in range(MODES):
-        parts = split3(qpad[pl.ds(m, LANES, stride=MODES), :])
-        for t in range(3):
-            qp[t, LANES * m : LANES * (m + 1), :] = parts[t]
-    wt[...] = jnp.zeros_like(wt)
-
-    row = lax.broadcasted_iota(jnp.int32, (8, LANES), 0)
-    blank = jnp.zeros((8, LANES), F32)
-
-    def store_modes(i, half, first_row, tile):
-        tile = jnp.where(row < MODES, tile, 0.0)
-        both = [blank, tile] if half else [tile, blank]
-        parts = split3(jnp.concatenate(both, axis=0))
-        for t in range(3):
-            wt[t, first_row : first_row + 16, LANES * i : LANES * (i + 1)] = parts[t]
-
-    for i in range(SLOTS):
-        store_modes(i, i // 8, 128, gown[i])
-
-    pending.append(exchange_wait(gsend, gall, 1))
-    ids = []
-    for i in range(SLOTS):
-        got = gall[pos[i]]
-        store_modes(i, i % 2, 16 * (i // 2), -got)
-        ids.append(jnp.broadcast_to(got[MODES : MODES + 1, :], (8, LANES)))
-    for s in range(2):
-        ids.append(jnp.full((8, LANES), cluster_ref[s].astype(F32), F32))
-
-    lane = lax.broadcasted_iota(jnp.int32, (16, LANES), 1)
-    mode = lax.broadcasted_iota(jnp.int32, (16, LANES), 0) & 7
-    lane_f = lane.astype(F32)
-    in_half = lane & 63
-    sub = (in_half * 43) >> 8
-    sub_mode = in_half - MODES * sub
-    fits = jnp.logical_and(in_half < 48, sub_mode == mode)
-    first_cluster = (sub + 8 * (lane >> 6)).astype(F32)
-    for a in range(9):
-        pair = jnp.concatenate([ids[2 * a], ids[2 * a + 1]], axis=0)
-        rows = slice(16 * a, 16 * (a + 1))
-        for m in range(MODES):
-            hit = jnp.logical_and(mode == m, lane_f == pair)
-            sc[rows, LANES * m : LANES * (m + 1)] = jnp.where(hit, 1.0, 0.0).astype(BF)
-        for j in range(8):
-            hit = jnp.logical_and(fits, first_cluster + 16.0 * j == pair)
-            scy[rows, LANES * j : LANES * (j + 1)] = jnp.where(hit, 1.0, 0.0).astype(BF)
 
     def pairs(ref):
         return jnp.concatenate(
             [ref[2 * j] + ref[2 * j + 1] for j in range(8)], axis=1
         )
 
-    def spread(y_slice, step):
-        y = yall.at[step]
-        r = 2 + step
-        y[mem] = y_slice
-        scatter(lambda peer: y.at[mem], y, r, "mem", mem, n_mem)
-        pending.append(finish(y, r, "mem", mem, n_mem))
-        picked = dot_exact(pairs(y), scy[...], nt=True)
-        return dot3(picked, (wt[0], wt[1], wt[2]))
+    def lanes_of(values, i):
+        return values[:, LANES * i : LANES * (i + 1)]
 
     def schur(src):
         out = []
@@ -247,47 +215,108 @@
             out.append(mm(flat, kbuf[s]))
         return out
 
-    def lanes_of(values, i):
-        return values[:, LANES * i : LANES * (i + 1)]
+    def lane_sum(x):
+        return jnp.sum(x, axis=1, keepdims=True)
+
+    lane8 = lax.broadcasted_iota(jnp.int32, (8, LANES), 1)
+    lane = lax.broadcasted_iota(jnp.int32, (CASES, LANES), 1)
+    low = lane8 < 64
 
     def reduce_start(step, scalars):
         t = (tall0, tall1, tall2)[step]
         e = eb.at[step]
         base = 6 + 4 * step
-        for i in range(SLOTS):
-            t[i] = town[step, i]
         flat = jnp.concatenate([town[step, i] for i in range(SLOTS)], axis=1)
         own = dot3(flat, (wt[0], wt[1], wt[2]), nt=True)
         dense = dot_exact(own, sc[...])
-        for m in range(MODES):
-            e[:, m, :] = lanes_of(dense, m)
+        extra = jnp.zeros((8, LANES), F32)
         for k, value in enumerate(scalars):
-            e[:, MODES + k, :] = value
+            value = lane_sum(value)
+            extra = jnp.where(lane8 == 48 + k, value[0:8], extra)
+            extra = jnp.where(lane8 == 112 + k, value[8:16], extra)
+        for j in range(8):
+            tile = lanes_of(dense, j)
+            up, down = tile[0:8], tile[8:16]
+            e[2 * j] = jnp.where(low, up, pltpu.roll(down, 64, 1)) + extra
+            e[2 * j + 1] = jnp.where(low, pltpu.roll(up, 64, 1), down) + extra
         rs[step, mem] = e[mem]
         scatter(lambda peer: e.at[peer], rs.at[step], base, "mem", mem, n_mem)
         for p in range(SLOTS):
             tsend[step, p] = town[step, sslot[p]]
         exchange_start(tsend.at[step], t, base + 1)
+        for i in range(SLOTS):
+            t[i] = town[step, i]
         pending.append(finish(rs.at[step], base, "mem", mem, n_mem))
         ra[step, rep] = total16(rs, step)
         scatter(lambda peer: ra.at[step, rep], ra.at[step], base + 2, "rep", rep, n_rep)
         pending.append(finish(ra.at[step], base + 2, "rep", rep, n_rep))
-        g = gb.at[step]
-        g[mem] = total16(ra, step)
-        scatter(lambda peer: g.at[mem], g, base + 3, "mem", mem, n_mem)
-        pending.append(finish(g, base + 3, "mem", mem, n_mem))
-        e_full = jnp.concatenate([g[:, m, :] for m in range(MODES)], axis=1)
-        z = spread(dot3(e_full, (qp[0], qp[1], qp[2])), 1 + step)
+        tile = total16(ra, step)
+        mine = jnp.concatenate([tile, pltpu.roll(tile, 64, 1)], axis=0)
+        product = dot3(mine, (ball[0], ball[1], ball[2]))
+        y = yall.at[1 + step]
+        out = ysend.at[step]
+        for m in range(16):
+            out[m] = lanes_of(product, m)
+        scatter(lambda peer: out.at[peer], y, base + 3, "mem", mem, n_mem)
+        y[mem] = out[mem]
         pending.append(exchange_wait(tsend.at[step], t, base + 1))
-        return [
-            (t[i] - t[pos[i]]) - lanes_of(z, i) for i in range(SLOTS)
+        image = [t[i] - t[pos[i]] for i in range(SLOTS)]
+        pending.append(finish(y, base + 3, "mem", mem, n_mem))
+        z = dot3(total16(yall, 1 + step), (wt[0], wt[1], wt[2]))
+        sums = [
+            jnp.concatenate([mine[0:8, k : k + 1], mine[8:16, k : k + 1]], axis=0)
+            for k in (48, 49)
         ]
-
-    def lane_sum(x):
-        return jnp.sum(x, axis=1, keepdims=True)
+        return [image[i] - lanes_of(z, i) for i in range(SLOTS)], sums
 
     pending.append(finish(crall, 0, "mem", mem, n_mem))
-    z = spread(dot3(pairs(crall), (qn[0], qn[1], qn[2])), 0)
+    y_slice = dot3(pairs(crall), (qp[0], qp[1], qp[2]), nt=True)
+    yall[0, mem] = y_slice
+    scatter(lambda peer: yall.at[0, mem], yall.at[0], 2, "mem", mem, n_mem)
+    pending.append(finish(rowall, 20, "mem", mem, n_mem))
+    cluster = jnp.full((16, LANES), -100.0, F32)
+    rows = jnp.concatenate([rowall[m] for m in range(16)], axis=0)
+    for m in range(16):
+        for s in range(2):
+            k = 6 * 18 + s
+            number = jnp.broadcast_to(rows[m : m + 1, k : k + 1], (16, LANES))
+            cluster = jnp.where(rows == 2.0 * m + s, number, cluster)
+    entry16 = (lane * 43) >> 8
+    mode16 = (lane - MODES * entry16).astype(F32)
+    index = jnp.where(entry16 < 18, 6.0 * cluster + mode16, -100.0)
+    for m in range(16):
+        index_ref[m] = index[m : m + 1]
+    column = jnp.transpose(jnp.broadcast_to(index_ref[mem], (LANES, LANES)))
+    in_half = lax.broadcasted_iota(jnp.int32, (LANES, LANES), 1)
+    whole = jnp.where(
+        (in_half & 63) < 48, 48 * (in_half >> 6) + (in_half & 63), -1
+    ).astype(F32)
+    for j in range(8):
+        hit = jnp.logical_and(whole >= 0.0, whole + 96.0 * j == column)
+        sc[:, LANES * j : LANES * (j + 1)] = jnp.where(hit, 1.0, 0.0).astype(BF)
+
+    pending.append(exchange_wait(gsend, gall, 1))
+    for i in range(SLOTS):
+        got = gall[pos[i]]
+        wtf[6 * i : 6 * i + 6, LANES * i : LANES * (i + 1)] = -got[0:MODES]
+    for i in range(SLOTS):
+        cut = slice(LANES * i, LANES * (i + 1))
+        parts = split3(wtf[:, cut])
+        for t in range(3):
+            wt[t, :, cut] = parts[t]
+
+    number = lax.broadcasted_iota(jnp.int32, (768, LANES), 0).astype(F32)
+    for m in range(16):
+        hit = number == jnp.broadcast_to(index_ref[m], (768, LANES))
+        chosen = mm(qs[...], jnp.where(hit, 1.0, 0.0).astype(BF))
+        for t in range(3):
+            ball[t, 0:48, LANES * m : LANES * (m + 1)] = (
+                chosen[48 * t : 48 * (t + 1)].astype(BF)
+            )
+
+    pending.append(finish(yall.at[0], 2, "mem", mem, n_mem))
+    picked = dot_exact(pairs(yall.at[0]), sc[...], nt=True)
+    z = dot3(picked, (wt[0], wt[1], wt[2]))
     for i in range(SLOTS):
         lam[i] = lanes_of(z, i)
     kcopy.wait()
@@ -297,7 +326,7 @@
         s, j = divmod(i, 8)
         cut = slice(LANES * j, LANES * (j + 1))
         town[0, i] = rhs_ref[:, s, cut] - terms[s][:, cut]
-    projected = reduce_start(0, (zero, zero))
+    projected, _ = reduce_start(0, ())
     square = zero
     for i in range(SLOTS):
         p0[i] = projected[i]
@@ -310,15 +339,13 @@
         value = terms[s][:, LANES * j : LANES * (j + 1)]
         town[1, i] = value
         curve = curve + value * p0[i]
-    image = reduce_start(1, (curve, square))
-    curvature = lane_sum(gb[1, :, MODES, :])
-    norm = 0.5 * lane_sum(gb[1, :, MODES + 1, :])
+    image, (curvature, norm) = reduce_start(1, (curve, square))
+    norm = 0.5 * norm
     alpha = norm / curvature
     square = zero
     for i in range(SLOTS):
         value = p0[i] - alpha * image[i]
         p1[i] = value
-        lam[i] = lam[i] + alpha * p0[i]
         square = square + value * value
     diagonal = lax.broadcasted_iota(jnp.int32, (CASES, LANES), 0) == lane
     as_row = jnp.sum(
@@ -326,6 +353,8 @@
     )
     tm[mem] = as_row
     scatter(lambda peer: tm.at[mem], tm, 18, "mem", mem, n_mem)
+    for i in range(SLOTS):
+        lam[i] = lam[i] + alpha * p0[i]
     pending.append(finish(tm, 18, "mem", mem, n_mem))
     tr[rep] = total16(tm)
     scatter(lambda peer: tr.at[rep], tr, 19, "rep", rep, n_rep)
@@ -344,8 +373,8 @@
         value = terms[s][:, LANES * j : LANES * (j + 1)]
         town[2, i] = value
         curve = curve + value * d1[i]
-    image = reduce_start(2, (curve, zero))
-    alpha = fresh / lane_sum(gb[2, :, MODES, :])
+    image, (curvature, _) = reduce_start(2, (curve,))
+    alpha = fresh / curvature
     for i in range(SLOTS):
         s, j = divmod(i, 8)
         cut = slice(LANES * j, LANES * (j + 1))
@@ -371,12 +400,13 @@
         out_specs=(vmem, vmem),
         scratch_shapes=[
             pltpu.VMEM((2, 1024, 1024), BF),
-            pltpu.VMEM((3, ENT, 2048), BF),
-            pltpu.VMEM((768, LANES), F32),
-            pltpu.VMEM((3, 768, LANES), BF),
-            pltpu.VMEM((3, 1024, LANES), BF),
-            pltpu.VMEM((ENT, 768), BF),
-            pltpu.VMEM((ENT, 1024), BF),
+            pltpu.VMEM((LANES, 2048), F32),
+            pltpu.VMEM((3, LANES, 2048), BF),
+            pltpu.VMEM((LANES, 1024), F32),
+            pltpu.VMEM((3, LANES, 1024), BF),
+            pltpu.VMEM((144, 768), BF),
+            pltpu.VMEM((3, LANES, 2048), BF),
+            pltpu.VMEM((LANES, 1024), BF),
             pltpu.VMEM((2 * SLOTS, 8, LANES), F32),
             pltpu.VMEM((SLOTS, 8, LANES), F32),
             pltpu.VMEM((SLOTS, 8, LANES), F32),
@@ -387,8 +417,10 @@
             pltpu.VMEM((STEPS, SLOTS, *tile), F32),
             pltpu.VMEM(tile, F32),
             pltpu.VMEM((16, *tile), F32),
+            pltpu.VMEM((16, 1, LANES), F32),
+            pltpu.VMEM((16, 1, LANES), F32),
             pltpu.VMEM((1 + STEPS, 16, *tile), F32),
-            pltpu.VMEM((STEPS, CASES, 8, LANES), F32),
+            pltpu.VMEM((STEPS, 16, *tile), F32),
             pltpu.VMEM((STEPS, 16, 8, LANES), F32),
             pltpu.VMEM((STEPS, 16, 8, LANES), F32),
             pltpu.VMEM((STEPS, 16, 8, LANES), F32),
@@ -403,15 +435,16 @@
             pltpu.SMEM((SLOTS,), jnp.int32),
             pltpu.SMEM((SLOTS,), jnp.int32),
             pltpu.SMEM((SLOTS,), F32),
+            pltpu.SMEM((SLOTS,), F32),
             pltpu.SemaphoreType.DMA,
-            pltpu.SemaphoreType.DMA((20,)),
-            pltpu.SemaphoreType.DMA((20,)),
+            pltpu.SemaphoreType.DMA((21,)),
+            pltpu.SemaphoreType.DMA((21,)),
         ],
         compiler_params=pltpu.CompilerParams(
             collective_id=0, has_side_effects=True, vmem_limit_bytes=60 * 1024 * 1024
         ),
     )(
-        partner, cluster_of, rigid_modes, coarse_inverse, coarse_rhs, subdomain_rhs,
+        partner, cluster_of, jnp.swapaxes(rigid_modes, 0, 1), coarse_inverse.T, coarse_rhs, subdomain_rhs,
         schur_blocks,
     )
 

time: 116 us -> 94.3 us (0.81)
  Pallas kernels: 109 us -> 90.4 us
  local copies, waits for them, and re-layouts: 6.39 us -> 3.14 us
    pallas_call x1, Pallas kernels: 109 us -> 90.4 us  [local(): pl.pallas_call(functools.partial(kernel, n_rep, n_mem), out_shape=(out, o...]
    unnamed x4 -> x2, local copies, waits for them, and re-layouts: 6.39 us -> 3.14 us
where the time goes in v2:
time: 94.3 us; the launch traced here: 94.2 us
  Pallas kernels  90.4 us (96%)
  local copies, waits for them, and re-layouts  3.14 us (3%)
    pallas_call x1, Pallas kernels, local(): pl.pallas_call(functools.partial(kernel, n_rep, n_mem), out_shape=(out, o...  90.4 us
    unnamed x2, local copies, waits for them, and re-layouts  3.14 us

profile of v2, /device:TPU:1, one launch (start us, length us, event | category | flops | bytes accessed | tf_op | source)
XLA Modules:
  0.0 94.2 jit_solution(15612055718322611325)
XLA Ops:
  0.6 90.4 %shard_map.86 = (f32[16,2,1024]{2,1,0:T(2,128)}, f32[16,2,1024]{2,1,0:T(2,128)}) custom-call(s32[2,8]{1,0:T(2,128)} %partner_ref.1, s32[2]{0:T(128)} %cluster_ref.1, f32[6,2,1024]{2,1,0:T(2,128)} %bitcast.3, f32[48,768]{1,0:T(8,128)} %bitcast.2, f32[16,48]{1,0:T(8,128)} %crhs_ref.1, f32[16,2,1024]{2,1,0:T(2,128)} %rhs_ref.1, bf16[2,1024,1024]{2,1,0:T(8,128)(2,1)} %schur_hbm.1), custom_call_target="tpu_custom_call" | custom-call | tf_op jit(solution)/shard_map/pallas_call | solution.py:396
  91.1 1.6 %copy.11 = f32[16,2,1024]{2,1,0:T(2,128)} copy(f32[16,2,1024]{2,1,0:T(2,128)} %get-tuple-element.4) | data formatting | bytes 262144
  92.6 1.6 %copy.12 = f32[16,2,1024]{2,1,0:T(2,128)} copy(f32[16,2,1024]{2,1,0:T(2,128)} %get-tuple-element.5) | data formatting | bytes 262144

commit v3 on v2

--- a/solution.py
+++ b/solution.py
@@ -55,11 +55,12 @@
 
 def kernel(
     n_rep, n_mem,
-    partner_ref, cluster_ref, modes_ref, qinv_ref, crhs_ref, rhs_ref, schur_hbm,
-    out_l, out_p,
+    partner_ref, cluster_ref, modes_hbm, qinv_hbm, crhs_hbm, rhs_hbm, schur_hbm,
+    outs,
+    modes_ref, qinv_ref, crhs_ref, rhs_ref,
     kbuf, wtf, wt, qf, qp, qs, ball, sc,
     gall, gown, gsend, tall0, tall1, tall2, town, tsend,
-    crpad, crall, rowall, index_ref, yall, ysend, eb, rs, ra,
+    crpad, crall, start, index_ref, yall, ysend, eb, rs, ra,
     tm, tr,
     lam, p0, p1, d1,
     key, code, pos, sslot, psub, sgn,
@@ -67,8 +68,6 @@
 ):
     rep = lax.axis_index("rep")
     mem = lax.axis_index("mem")
-    kcopy = pltpu.make_async_copy(schur_hbm, kbuf, ksem)
-    kcopy.start()
     bar = pltpu.get_barrier_semaphore()
 
     def greet(axis, me, n):
@@ -81,6 +80,16 @@
 
     greet("mem", mem, n_mem)
     greet("rep", rep, n_rep)
+    inputs = [
+        pltpu.make_async_copy(modes_hbm, modes_ref, ksem.at[0]),
+        pltpu.make_async_copy(crhs_hbm, crhs_ref, ksem.at[1]),
+        pltpu.make_async_copy(qinv_hbm, qinv_ref, ksem.at[2]),
+        pltpu.make_async_copy(rhs_hbm, rhs_ref, ksem.at[3]),
+    ]
+    for copy in inputs:
+        copy.start()
+    kcopy = pltpu.make_async_copy(schur_hbm, kbuf, ksem.at[4])
+    kcopy.start()
 
     def remote(src, dst, r, axis, peer):
         return pltpu.make_async_remote_copy(
@@ -149,6 +158,7 @@
         return 0
     lax.fori_loop(0, SLOTS, places, 0)
 
+    inputs[0].wait()
     for i in range(SLOTS):
         s, j = divmod(i, 8)
         value = modes_ref[:, s, LANES * j : LANES * (j + 1)]
@@ -157,29 +167,39 @@
     for p in range(SLOTS):
         gsend[p] = gown[sslot[p]]
 
-    lane1 = lax.broadcasted_iota(jnp.int32, (1, LANES), 1)
-    entry = (lane1 * 43) >> 8
-    row = jnp.full((1, LANES), -1.0, F32)
-    for i in range(SLOTS):
-        row = jnp.where(entry == i, psub[i], row)
+    lane8 = lax.broadcasted_iota(jnp.int32, (8, LANES), 1)
+    lane = lax.broadcasted_iota(jnp.int32, (CASES, LANES), 1)
+    low = lane8 < 64
+
+    def pack(x):
+        return jnp.where(low, x[0:8], pltpu.roll(x[8:16], 64, 1))
+
+    def unpack(ref):
+        out = []
+        for j in range(8):
+            left, right = ref[2 * j], ref[2 * j + 1]
+            up = jnp.where(low, left, pltpu.roll(right, 64, 1))
+            down = jnp.where(low, pltpu.roll(left, 64, 1), right)
+            out.append(jnp.concatenate([up, down], axis=0))
+        return jnp.concatenate(out, axis=1)
+
+    crpad[...] = jnp.zeros_like(crpad)
+    inputs[1].wait()
+    crpad[:, 0:48] = crhs_ref[...]
+    place = pack(crpad[...])
+    for i in range(SLOTS):
+        place = jnp.where(lane8 == 48 + i, psub[i], place)
     for s in range(2):
-        row = jnp.where(entry == SLOTS + s, (2 * mem + s).astype(F32), row)
-        row = jnp.where(lane1 == 6 * 18 + s, cluster_ref[s].astype(F32), row)
-    rowall[mem] = row
-
-    odd = (mem & 1) == 1
-    crpad[...] = jnp.zeros_like(crpad)
-    crpad[:, 0:48] = crhs_ref[...]
-    place = crpad[...]
-    crall[mem] = jnp.where(odd, pltpu.roll(place, 64, 1), place)
-
+        place = jnp.where(lane8 == 112 + s, cluster_ref[s].astype(F32), place)
+    crall[mem] = place
+
+    inputs[2].wait()
     parts = split3(qinv_ref[...])
     for t in range(3):
         qs[48 * t : 48 * (t + 1), :] = parts[t]
     qf[...] = jnp.zeros_like(qf)
-    half = pl.ds(pl.multiple_of(64 * (mem & 1), 64), 48)
     for m in range(16):
-        qf[half, 64 * m : 64 * m + 48] = qinv_ref[:, 48 * m : 48 * (m + 1)]
+        qf[0:48, 64 * m : 64 * m + 48] = qinv_ref[:, 48 * m : 48 * (m + 1)]
     for j in range(8):
         cut = slice(LANES * j, LANES * (j + 1))
         parts = split3(qf[:, cut])
@@ -195,13 +215,7 @@
 
     pending = []
     scatter(lambda peer: crall.at[mem], crall, 0, "mem", mem, n_mem)
-    scatter(lambda peer: rowall.at[mem], rowall, 20, "mem", mem, n_mem)
     exchange_start(gsend, gall, 1)
-
-    def pairs(ref):
-        return jnp.concatenate(
-            [ref[2 * j] + ref[2 * j + 1] for j in range(8)], axis=1
-        )
 
     def lanes_of(values, i):
         return values[:, LANES * i : LANES * (i + 1)]
@@ -217,10 +231,6 @@
 
     def lane_sum(x):
         return jnp.sum(x, axis=1, keepdims=True)
-
-    lane8 = lax.broadcasted_iota(jnp.int32, (8, LANES), 1)
-    lane = lax.broadcasted_iota(jnp.int32, (CASES, LANES), 1)
-    low = lane8 < 64
 
     def reduce_start(step, scalars):
         t = (tall0, tall1, tall2)[step]
@@ -237,23 +247,23 @@
         for j in range(8):
             tile = lanes_of(dense, j)
             up, down = tile[0:8], tile[8:16]
-            e[2 * j] = jnp.where(low, up, pltpu.roll(down, 64, 1)) + extra
+            e[2 * j] = pack(tile) + extra
             e[2 * j + 1] = jnp.where(low, pltpu.roll(up, 64, 1), down) + extra
         rs[step, mem] = e[mem]
         scatter(lambda peer: e.at[peer], rs.at[step], base, "mem", mem, n_mem)
         for p in range(SLOTS):
             tsend[step, p] = town[step, sslot[p]]
-        exchange_start(tsend.at[step], t, base + 1)
         for i in range(SLOTS):
             t[i] = town[step, i]
         pending.append(finish(rs.at[step], base, "mem", mem, n_mem))
         ra[step, rep] = total16(rs, step)
         scatter(lambda peer: ra.at[step, rep], ra.at[step], base + 2, "rep", rep, n_rep)
+        exchange_start(tsend.at[step], t, base + 1)
         pending.append(finish(ra.at[step], base + 2, "rep", rep, n_rep))
         tile = total16(ra, step)
         mine = jnp.concatenate([tile, pltpu.roll(tile, 64, 1)], axis=0)
         product = dot3(mine, (ball[0], ball[1], ball[2]))
-        y = yall.at[1 + step]
+        y = yall.at[step]
         out = ysend.at[step]
         for m in range(16):
             out[m] = lanes_of(product, m)
@@ -262,7 +272,7 @@
         pending.append(exchange_wait(tsend.at[step], t, base + 1))
         image = [t[i] - t[pos[i]] for i in range(SLOTS)]
         pending.append(finish(y, base + 3, "mem", mem, n_mem))
-        z = dot3(total16(yall, 1 + step), (wt[0], wt[1], wt[2]))
+        z = dot3(total16(yall, step), (wt[0], wt[1], wt[2]))
         sums = [
             jnp.concatenate([mine[0:8, k : k + 1], mine[8:16, k : k + 1]], axis=0)
             for k in (48, 49)
@@ -270,16 +280,23 @@
         return [image[i] - lanes_of(z, i) for i in range(SLOTS)], sums
 
     pending.append(finish(crall, 0, "mem", mem, n_mem))
-    y_slice = dot3(pairs(crall), (qp[0], qp[1], qp[2]), nt=True)
-    yall[0, mem] = y_slice
-    scatter(lambda peer: yall.at[0, mem], yall.at[0], 2, "mem", mem, n_mem)
-    pending.append(finish(rowall, 20, "mem", mem, n_mem))
+    y_slice = dot3(unpack(crall), (qp[0], qp[1], qp[2]), nt=True)
+    start[mem] = pack(y_slice)
+    scatter(lambda peer: start.at[mem], start, 2, "mem", mem, n_mem)
+    heads = jnp.concatenate([crall[m][0:1] for m in range(16)], axis=0)
+    source = lax.broadcasted_iota(jnp.int32, (LANES, LANES), 0)
+    wanted = 48 + ((lax.broadcasted_iota(jnp.int32, (LANES, LANES), 1) * 43) >> 8)
+    widen = jnp.where(source == wanted, 1.0, 0.0).astype(BF)
+    rows = mm(heads.astype(BF), widen)
+    member = 2 * lax.broadcasted_iota(jnp.int32, (16, LANES), 0).astype(F32)
+    for s in range(2):
+        own_lane = ((lane * 43) >> 8) == SLOTS + s
+        rows = jnp.where(own_lane, member + float(s), rows)
     cluster = jnp.full((16, LANES), -100.0, F32)
-    rows = jnp.concatenate([rowall[m] for m in range(16)], axis=0)
     for m in range(16):
         for s in range(2):
-            k = 6 * 18 + s
-            number = jnp.broadcast_to(rows[m : m + 1, k : k + 1], (16, LANES))
+            k = 112 + s
+            number = jnp.broadcast_to(heads[m : m + 1, k : k + 1], (16, LANES))
             cluster = jnp.where(rows == 2.0 * m + s, number, cluster)
     entry16 = (lane * 43) >> 8
     mode16 = (lane - MODES * entry16).astype(F32)
@@ -314,11 +331,12 @@
                 chosen[48 * t : 48 * (t + 1)].astype(BF)
             )
 
-    pending.append(finish(yall.at[0], 2, "mem", mem, n_mem))
-    picked = dot_exact(pairs(yall.at[0]), sc[...], nt=True)
+    pending.append(finish(start, 2, "mem", mem, n_mem))
+    picked = dot_exact(unpack(start), sc[...], nt=True)
     z = dot3(picked, (wt[0], wt[1], wt[2]))
     for i in range(SLOTS):
         lam[i] = lanes_of(z, i)
+    inputs[3].wait()
     kcopy.wait()
     zero = jnp.zeros((CASES, LANES), F32)
     terms = schur(lam)
@@ -378,8 +396,8 @@
     for i in range(SLOTS):
         s, j = divmod(i, 8)
         cut = slice(LANES * j, LANES * (j + 1))
-        out_l[:, s, cut] = sgn[i] * (lam[i] + alpha * d1[i])
-        out_p[:, s, cut] = sgn[i] * (p1[i] - alpha * image[i])
+        outs[0, :, s, cut] = sgn[i] * (lam[i] + alpha * d1[i])
+        outs[1, :, s, cut] = sgn[i] * (p1[i] - alpha * image[i])
 
     for copy in pending:
         copy.wait_send()
@@ -391,14 +409,18 @@
 ):
     vmem = pl.BlockSpec(memory_space=pltpu.VMEM)
     smem = pl.BlockSpec(memory_space=pltpu.SMEM)
-    out = jax.ShapeDtypeStruct((CASES, 2, 1024), F32)
+    out = jax.ShapeDtypeStruct((2, CASES, 2, 1024), F32)
     tile = (CASES, LANES)
-    return pl.pallas_call(
+    found = pl.pallas_call(
         functools.partial(kernel, n_rep, n_mem),
-        out_shape=(out, out),
-        in_specs=[smem, smem, vmem, vmem, vmem, vmem, pl.BlockSpec(memory_space=pl.ANY)],
-        out_specs=(vmem, vmem),
+        out_shape=out,
+        in_specs=[smem, smem] + [pl.BlockSpec(memory_space=pl.ANY)] * 5,
+        out_specs=vmem,
         scratch_shapes=[
+            pltpu.VMEM((MODES, 2, 1024), F32),
+            pltpu.VMEM((48, 768), F32),
+            pltpu.VMEM((CASES, 48), F32),
+            pltpu.VMEM((CASES, 2, 1024), F32),
             pltpu.VMEM((2, 1024, 1024), BF),
             pltpu.VMEM((LANES, 2048), F32),
             pltpu.VMEM((3, LANES, 2048), BF),
@@ -407,19 +429,19 @@
             pltpu.VMEM((144, 768), BF),
             pltpu.VMEM((3, LANES, 2048), BF),
             pltpu.VMEM((LANES, 1024), BF),
-            pltpu.VMEM((2 * SLOTS, 8, LANES), F32),
-            pltpu.VMEM((SLOTS, 8, LANES), F32),
-            pltpu.VMEM((SLOTS, 8, LANES), F32),
+            pltpu.VMEM((2 * SLOTS, MODES, LANES), F32),
+            pltpu.VMEM((SLOTS, MODES, LANES), F32),
+            pltpu.VMEM((SLOTS, MODES, LANES), F32),
             pltpu.VMEM((2 * SLOTS, *tile), F32),
             pltpu.VMEM((2 * SLOTS, *tile), F32),
             pltpu.VMEM((2 * SLOTS, *tile), F32),
             pltpu.VMEM((STEPS, SLOTS, *tile), F32),
             pltpu.VMEM((STEPS, SLOTS, *tile), F32),
             pltpu.VMEM(tile, F32),
-            pltpu.VMEM((16, *tile), F32),
+            pltpu.VMEM((16, 8, LANES), F32),
+            pltpu.VMEM((16, 8, LANES), F32),
             pltpu.VMEM((16, 1, LANES), F32),
-            pltpu.VMEM((16, 1, LANES), F32),
-            pltpu.VMEM((1 + STEPS, 16, *tile), F32),
+            pltpu.VMEM((STEPS, 16, *tile), F32),
             pltpu.VMEM((STEPS, 16, *tile), F32),
             pltpu.VMEM((STEPS, 16, 8, LANES), F32),
             pltpu.VMEM((STEPS, 16, 8, LANES), F32),
@@ -436,9 +458,9 @@
             pltpu.SMEM((SLOTS,), jnp.int32),
             pltpu.SMEM((SLOTS,), F32),
             pltpu.SMEM((SLOTS,), F32),
-            pltpu.SemaphoreType.DMA,
-            pltpu.SemaphoreType.DMA((21,)),
-            pltpu.SemaphoreType.DMA((21,)),
+            pltpu.SemaphoreType.DMA((5,)),
+            pltpu.SemaphoreType.DMA((20,)),
+            pltpu.SemaphoreType.DMA((20,)),
         ],
         compiler_params=pltpu.CompilerParams(
             collective_id=0, has_side_effects=True, vmem_limit_bytes=60 * 1024 * 1024
@@ -447,6 +469,7 @@
         partner, cluster_of, jnp.swapaxes(rigid_modes, 0, 1), coarse_inverse.T, coarse_rhs, subdomain_rhs,
         schur_blocks,
     )
+    return found[0], found[1]
 
 
 def solution(mesh):

time: 94.3 us -> 88.5 us (0.938)
  Pallas kernels: 90.4 us -> 86.1 us
  local copies, waits for them, and re-layouts: 3.14 us -> 1.69 us
    pallas_call x1, Pallas kernels: 90.4 us -> 86.1 us  [local(): pl.pallas_call(functools.partial(kernel, n_rep, n_mem), out_shape=out, in...]
    unnamed x2 -> x0, local copies, waits for them, and re-layouts: 3.14 us -> none
    squeeze x0 -> x1, local copies, waits for them, and re-layouts: none -> 1.69 us  [local(): return (found[0], found[1])]
where the time goes in v3:
time: 88.5 us; the launch traced here: 88.4 us
  Pallas kernels  86.1 us (97%)
  local copies, waits for them, and re-layouts  1.69 us (2%)
    pallas_call x1, Pallas kernels, local(): pl.pallas_call(functools.partial(kernel, n_rep, n_mem), out_shape=out, in...  86.1 us

profile of v3, /device:TPU:1, one launch (start us, length us, event | category | flops | bytes accessed | tf_op | source)
XLA Modules:
  0.0 88.4 jit_solution(8029848351229796767)
XLA Ops:
  0.6 86.1 %shard_map.86 = f32[2,16,2,1024]{3,2,1,0:T(2,128)} custom-call(s32[2,8]{1,0:T(2,128)} %partner_ref.1, s32[2]{0:T(128)} %cluster_ref.1, f32[6,2,1024]{2,1,0:T(2,128)} %bitcast.7, f32[48,768]{1,0:T(8,128)} %bitcast.6, f32[16,48]{1,0:T(8,128)} %crhs_hbm.1, f32[16,2,1024]{2,1,0:T(2,128)} %rhs_hbm.1, bf16[2,1024,1024]{2,1,0:T(8,128)(2,1)} %schur_hbm.1), custom_call_target="tpu_custom_call" | custom-call | tf_op jit(solution)/shard_map/pallas_call | solution.py:414
  86.7 1.7 %slice_bitcast_fusion = (f32[16,2,1024]{2,1,0:T(2,128)}, f32[16,2,1024]{2,1,0:T(2,128)}) fusion(f32[2,16,2,1024]{3,2,1,0:T(2,128)} %shard_map.86), kind=kLoop, calls=%fused_computation | loop fusion | bytes 524288 | tf_op jit(solution)/shard_map/squeeze | solution.py:472

commit v4 on v3

--- a/solution.py
+++ b/solution.py
@@ -68,6 +68,7 @@
 ):
     rep = lax.axis_index("rep")
     mem = lax.axis_index("mem")
+    far = 1 - (mem >> 3)
     bar = pltpu.get_barrier_semaphore()
 
     def greet(axis, me, n):
@@ -97,12 +98,12 @@
             device_id={axis: peer}, device_id_type=MESH,
         )
 
-    def scatter(src_of, dst, r, axis, me, n):
+    def scatter(src_of, dst, r, axis, me, n, first=1, last=16):
         def body(k, _):
             peer = me ^ (n - k)
             remote(src_of(peer), dst.at[me], r, axis, peer).start()
             return 0
-        lax.fori_loop(1, n, body, 0)
+        lax.fori_loop(first, min(n, last), body, 0, unroll=3)
 
     def finish(dst, r, axis, me, n):
         most = dst.at[pl.ds(0, n - 1)]
@@ -238,19 +239,25 @@
         base = 6 + 4 * step
         flat = jnp.concatenate([town[step, i] for i in range(SLOTS)], axis=1)
         own = dot3(flat, (wt[0], wt[1], wt[2]), nt=True)
-        dense = dot_exact(own, sc[...])
         extra = jnp.zeros((8, LANES), F32)
         for k, value in enumerate(scalars):
             value = lane_sum(value)
             extra = jnp.where(lane8 == 48 + k, value[0:8], extra)
             extra = jnp.where(lane8 == 112 + k, value[8:16], extra)
-        for j in range(8):
-            tile = lanes_of(dense, j)
-            up, down = tile[0:8], tile[8:16]
-            e[2 * j] = pack(tile) + extra
-            e[2 * j + 1] = jnp.where(low, pltpu.roll(up, 64, 1), down) + extra
+        for part, first, last in ((far, 1, 9), (1 - far, 9, 16)):
+            cut = pl.ds(pl.multiple_of(512 * part, 512), 512)
+            dense = dot_exact(own, sc[:, cut])
+            for j in range(4):
+                tile = lanes_of(dense, j)
+                up, down = tile[0:8], tile[8:16]
+                e[8 * part + 2 * j] = pack(tile) + extra
+                e[8 * part + 2 * j + 1] = (
+                    jnp.where(low, pltpu.roll(up, 64, 1), down) + extra
+                )
+            scatter(
+                lambda peer: e.at[peer], rs.at[step], base, "mem", mem, n_mem, first, last
+            )
         rs[step, mem] = e[mem]
-        scatter(lambda peer: e.at[peer], rs.at[step], base, "mem", mem, n_mem)
         for p in range(SLOTS):
             tsend[step, p] = town[step, sslot[p]]
         for i in range(SLOTS):
@@ -262,12 +269,16 @@
         pending.append(finish(ra.at[step], base + 2, "rep", rep, n_rep))
         tile = total16(ra, step)
         mine = jnp.concatenate([tile, pltpu.roll(tile, 64, 1)], axis=0)
-        product = dot3(mine, (ball[0], ball[1], ball[2]))
         y = yall.at[step]
         out = ysend.at[step]
-        for m in range(16):
-            out[m] = lanes_of(product, m)
-        scatter(lambda peer: out.at[peer], y, base + 3, "mem", mem, n_mem)
+        for part, first, last in ((far, 1, 9), (1 - far, 9, 16)):
+            cut = pl.ds(pl.multiple_of(1024 * part, 1024), 1024)
+            product = dot3(mine, (ball[0, :, cut], ball[1, :, cut], ball[2, :, cut]))
+            for m in range(8):
+                out[8 * part + m] = lanes_of(product, m)
+            scatter(
+                lambda peer: out.at[peer], y, base + 3, "mem", mem, n_mem, first, last
+            )
         y[mem] = out[mem]
         pending.append(exchange_wait(tsend.at[step], t, base + 1))
         image = [t[i] - t[pos[i]] for i in range(SLOTS)]

time: 88.5 us -> 87.7 us (level)
  Pallas kernels: 86.1 us -> 85.2 us
where the time goes in v4:
time: 87.7 us; the launch traced here: 87.6 us
  Pallas kernels  85.2 us (97%)
  local copies, waits for them, and re-layouts  1.69 us (2%)
    pallas_call x1, Pallas kernels, local(): pl.pallas_call(functools.partial(kernel, n_rep, n_mem), out_shape=out, in...  85.2 us

profile of v4, /device:TPU:1, one launch (start us, length us, event | category | flops | bytes accessed | tf_op | source)
XLA Modules:
  0.0 87.6 jit_solution(6038570523485541760)
XLA Ops:
  0.6 85.2 %shard_map.86 = f32[2,16,2,1024]{3,2,1,0:T(2,128)} custom-call(s32[2,8]{1,0:T(2,128)} %partner_ref.1, s32[2]{0:T(128)} %cluster_ref.1, f32[6,2,1024]{2,1,0:T(2,128)} %bitcast.7, f32[48,768]{1,0:T(8,128)} %bitcast.6, f32[16,48]{1,0:T(8,128)} %crhs_hbm.1, f32[16,2,1024]{2,1,0:T(2,128)} %rhs_hbm.1, bf16[2,1024,1024]{2,1,0:T(8,128)(2,1)} %schur_hbm.1), custom_call_target="tpu_custom_call" | custom-call | tf_op jit(solution)/shard_map/pallas_call | solution.py:425
  85.9 1.7 %slice_bitcast_fusion = (f32[16,2,1024]{2,1,0:T(2,128)}, f32[16,2,1024]{2,1,0:T(2,128)}) fusion(f32[2,16,2,1024]{3,2,1,0:T(2,128)} %shard_map.86), kind=kLoop, calls=%fused_computation | loop fusion | bytes 524288 | tf_op jit(solution)/shard_map/squeeze | solution.py:483
